TPU v7x, 512 devices: a whole 4x4x16 slice. The times are simulated.
512 devices in a mesh: guide: 2 (over core), dp: 16 (over y, x), mp: 16 (over z).
Axes of the slice: x: 4, y: 4, z: 16, core: 2. Of those that a mesh axis runs over, the one named last changes fastest.
Arguments:
- states: bfloat16 [2, 128, 2048], P('guide', 'dp'), may hold values from -6 to 6
- lengths: int32 [2, 128], P('guide', 'dp'), may hold values from 1 to 32768, as said below
- sink_cache: bfloat16 [2, 128, 16, 2, 4, 128], P('guide', 'dp', 'mp'), may hold values from -48 to 48
- window_cache: bfloat16 [2, 128, 16, 2, 256, 128], P('guide', 'dp', 'mp'), may hold values from -360 to 360
- qkv_weight: bfloat16 [2048, 3, 16, 128], P(None, None, 'mp'), may hold values from -0.125 to 0.125
- out_weight: bfloat16 [16, 128, 2048], P('mp'), may hold values from -0.125 to 0.125
- expert_ids: int32 [2, 128, 8], replicated, may hold values from 0 to 63, all different within a row; in each aligned block of 8 rows (0 to 7, 8 to 15, ..., all dimensions but the last counted through in order) at most 2 rows name the same one
- route_weight: float32 [2, 128, 8], replicated, may hold values from 0.5 to 2
- expert_in: bfloat16 [2, 2048, 65536], P(None, None, ('guide', 'dp', 'mp')), may hold values from -0.125 to 0.125
- expert_out: bfloat16 [65536, 2048], P(('guide', 'dp', 'mp')), may hold values from -0.1875 to 0.1875
- vocab_weight: bfloat16 [2048, 26624], P(('guide', 'dp'), 'mp'), may hold values from -0.125 to 0.125
- guidance: float32 [128], P('dp'), may hold values from 1 to 5
Outputs:
- guided: float32 [128, 16, 2, 832], P('dp', 'mp', 'guide')
Inputs may be any that keep to these rules, and one draw needn't show every extreme that they name: `lengths`: one stream of one request has exactly 32768 cached positions. `expert_ids`: taking the tokens streams first, then requests, in aligned blocks of 8 tokens (the tokens of one device), no expert is named by more than 2 tokens of a block, a bound that some block reaches.
All inputs are finite; a program needn't handle non-finite values.
Results may differ from a plain program's by a relative error of at most 0.025.
Values may be sent and summed in bfloat16 or wider, within the bound.
A program may use at most 64 MiB of HBM per device.

v0:
```python
import math
import jax
import jax.numpy as jnp
from jax import lax
from jax.sharding import PartitionSpec as P

FFE = 1024
EPSILON = 1e-05


def partner(block, axis, stride):
    count = lax.axis_size(axis)
    route = []
    for low in range(count):
        high = low | 1 << stride
        if high != low and high < count:
            route += [(low, high), (high, low)]
    return lax.ppermute(block, axis, route)


def rms_norm(values):
    return values * lax.rsqrt(jnp.mean(values * values, axis=-1, keepdims=True) + EPSILON)


def rotate(vectors, positions):
    full_width = vectors.shape[-1]
    half_width = full_width // 2
    step_index = jnp.arange(half_width, dtype=jnp.float32)
    inverse = jnp.exp(step_index * (-2.0 * math.log(10000.0) / full_width))
    angles = positions.astype(jnp.float32)[:, None] * inverse[None, :]
    cosine = jnp.cos(angles)[:, None, :]
    sine_part = jnp.sin(angles)[:, None, :]
    first_half = vectors[..., :half_width]
    second = vectors[..., half_width:]
    return jnp.concatenate(
        [first_half * cosine - second * sine_part, second * cosine + first_half * sine_part],
        axis=-1,
    )


def body(
    states,
    lengths,
    sink_cache,
    window_cache,
    qkv_weight,
    out_weight,
    expert_ids,
    route_weight,
    expert_in,
    expert_out,
    vocab_weight,
    guidance,
):
    hidden = states[0]
    own_lengths = lengths[0]
    request_count = hidden.shape[0]
    normed = rms_norm(hidden.astype(jnp.float32)).astype(jnp.bfloat16)
    projected = jnp.einsum("rd,dthe->rthe", normed, qkv_weight, preferred_element_type=jnp.float32)
    query_rot = rotate(projected[:, 0], own_lengths).astype(jnp.bfloat16)
    fresh_key = rotate(projected[:, 1], own_lengths).astype(jnp.bfloat16)
    fresh_value = projected[:, 2].astype(jnp.bfloat16)
    sink_rows = sink_cache[0]
    window_rows = window_cache[0]
    sink_count = sink_rows.shape[3]
    window_count = window_rows.shape[3]
    root_size = math.sqrt(query_rot.shape[-1])
    sink_scores = (
        jnp.einsum(
            "rhe,rhse->rhs", query_rot, sink_rows[:, :, 0], preferred_element_type=jnp.float32
        )
        / root_size
    )
    window_scores = (
        jnp.einsum(
            "rhe,rhwe->rhw", query_rot, window_rows[:, :, 0], preferred_element_type=jnp.float32
        )
        / root_size
    )
    self_scores = (
        jnp.einsum("rhe,rhe->rh", query_rot, fresh_key, preferred_element_type=jnp.float32)
        / root_size
    )
    length_limit = own_lengths[:, None, None]
    sink_valid = jnp.arange(sink_count, dtype=jnp.int32)[None, None, :] < length_limit
    window_valid = (
        jnp.arange(window_count, dtype=jnp.int32)[None, None, :]
        >= sink_count + window_count - length_limit
    )
    sink_scores = jnp.where(sink_valid, sink_scores, -1e30)
    window_scores = jnp.where(window_valid, window_scores, -1e30)
    highest = jnp.maximum(
        jnp.maximum(jnp.max(sink_scores, axis=-1), jnp.max(window_scores, axis=-1)), self_scores
    )
    sink_exp = jnp.exp(sink_scores - highest[..., None])
    window_exp = jnp.exp(window_scores - highest[..., None])
    self_exp = jnp.exp(self_scores - highest)
    totals = jnp.sum(sink_exp, axis=-1) + jnp.sum(window_exp, axis=-1) + self_exp
    sink_prob = (sink_exp / totals[..., None]).astype(jnp.bfloat16)
    window_prob = (window_exp / totals[..., None]).astype(jnp.bfloat16)
    self_prob = (self_exp / totals).astype(jnp.bfloat16)
    mixture = (
        jnp.einsum(
            "rhs,rhse->rhe", sink_prob, sink_rows[:, :, 1], preferred_element_type=jnp.float32
        )
        + jnp.einsum(
            "rhw,rhwe->rhe", window_prob, window_rows[:, :, 1], preferred_element_type=jnp.float32
        )
        + self_prob[..., None].astype(jnp.float32) * fresh_value.astype(jnp.float32)
    ).astype(jnp.bfloat16)
    partial_out = jnp.einsum("rhe,hed->rd", mixture, out_weight, preferred_element_type=jnp.float32)
    attention_out = lax.psum(partial_out, "mp")
    residual = (hidden.astype(jnp.float32) + attention_out).astype(jnp.bfloat16)
    moe_in = rms_norm(residual.astype(jnp.float32)).astype(jnp.bfloat16)
    unit_count = expert_in.shape[2]
    unit_start = lax.axis_index(("guide", "dp", "mp")) * unit_count
    unit_expert = (unit_start + jnp.arange(unit_count, dtype=jnp.int32)) // FFE
    choice_rows = expert_ids.reshape(-1, expert_ids.shape[-1])
    route_rows = route_weight.reshape(-1, route_weight.shape[-1])
    coefficient = jnp.sum(
        jnp.where(
            choice_rows[:, :, None] == unit_expert[None, None, :], route_rows[:, :, None], 0.0
        ),
        axis=1,
    )
    piece = lax.all_gather(moe_in, ("guide", "dp"), axis=0, tiled=True)
    gate = jnp.dot(piece, expert_in[0], preferred_element_type=jnp.float32)
    upward = jnp.dot(piece, expert_in[1], preferred_element_type=jnp.float32)
    activated = (jax.nn.silu(gate) * upward * coefficient).astype(jnp.bfloat16)
    expert_terms = jnp.dot(activated, expert_out, preferred_element_type=jnp.float32)
    expert_part = lax.psum_scatter(expert_terms, ("guide", "dp"), scatter_dimension=0, tiled=True)
    expert_total = lax.psum(expert_part, "mp")
    final = rms_norm(residual.astype(jnp.float32) + expert_total).astype(jnp.bfloat16)
    final_all = lax.all_gather(final, ("guide", "dp"), axis=0, tiled=True)
    row_share = vocab_weight.shape[0]
    share_start = lax.axis_index(("guide", "dp")) * row_share
    final_cols = lax.dynamic_slice_in_dim(final_all, share_start, row_share, 1)
    logits = lax.psum_scatter(
        jnp.dot(final_cols, vocab_weight, preferred_element_type=jnp.float32).astype(jnp.bfloat16),
        ("guide", "dp"),
        scatter_dimension=0,
        tiled=True,
    ).astype(jnp.float32)
    half_width = logits.shape[1] // 2
    stream_index = lax.axis_index("guide")
    own_half = lax.dynamic_slice_in_dim(logits, stream_index * half_width, half_width, 1)
    other_half = lax.dynamic_slice_in_dim(logits, (1 - stream_index) * half_width, half_width, 1)
    partner_logits = partner(other_half, "guide", 0)
    is_conditional = stream_index == 0
    conditional = jnp.where(is_conditional, own_half, partner_logits)
    unconditional = jnp.where(is_conditional, partner_logits, own_half)
    guided = unconditional + guidance[:, None] * (conditional - unconditional)
    return guided.reshape(request_count, 1, 1, half_width)


def solution(mesh):
    in_specs = (
        P("guide", "dp", None),
        P("guide", "dp"),
        P("guide", "dp", "mp", None, None, None),
        P("guide", "dp", "mp", None, None, None),
        P(None, None, "mp", None),
        P("mp", None, None),
        P(),
        P(),
        P(None, None, ("guide", "dp", "mp")),
        P(("guide", "dp", "mp"), None),
        P(("guide", "dp"), "mp"),
        P("dp"),
    )
    out_specs = P("dp", "mp", "guide", None)
    return jax.shard_map(body, mesh=mesh, in_specs=in_specs, out_specs=out_specs, check_vma=False)
```

profile of v0, /device:TPU:1, one launch (start us, length us, event | category | flops | bytes accessed | tf_op | source)
XLA Modules:
  0.0 657.1 jit_solution(2036525778644055514)
XLA Ops:
  6.6 0.8 bitcast_convert_fusion
  7.4 0.8 broadcast_subtract_fusion
  8.2 0.9 fusion.23
  9.1 1.2 fusion
  12.1 0.9 fusion.11
  13.0 128.0 %all-reduce.5.cloned.1.call-done = f32[8,2048]{1,0:T(8,128)} async-done(((f32[8,2048]{1,0:T(8,128)}), f32[8,2048]{1,0:T(8,128)}) %all-reduce.5.cloned.1.call-update) | async-done | bytes 65552 | tf_op jit(solution)/shard_map/psum | solution.py:112
  141.0 1.0 fusion.26
  142.0 0.7 fusion.27
  143.1 1.3 select_reduce_fusion
  144.4 65.6 %all-gather.3.cloned.1.call-done = bf16[256,2048]{1,0:T(8,128)(2,1)} async-done(((bf16[8,2048]{1,0:T(8,128)(2,1)}), bf16[256,2048]{1,0:T(8,128)(2,1)}) %all-gather.3.cloned.1.call-update) | async-done | bytes 1048592 | tf_op jit(solution)/shard_map/all_gather | solution.py:126
  210.0 1.9 fusion.9
  211.9 3.2 fusion.4
  215.2 99.4 %reduce-scatter.2.cloned.1.call-done = f32[8,2048]{1,0:T(8,128)} async-done(((f32[256,2048]{1,0:T(8,128)}), f32[8,2048]{1,0:T(8,128)}) %reduce-scatter.2.cloned.1.call-update) | async-done | bytes 65552 | tf_op jit(solution)/shard_map/reduce_scatter | solution.py:131
  314.6 125.9 %all-reduce.7.cloned.1.call-done = f32[8,2048]{1,0:T(8,128)} async-done(((f32[8,2048]{1,0:T(8,128)}), f32[8,2048]{1,0:T(8,128)}) %all-reduce.7.cloned.1.call-update) | async-done | bytes 65552 | tf_op jit(solution)/shard_map/psum | solution.py:132
  440.5 1.0 multiply_reduce_fusion
  441.5 1.5 multiply_convert_fusion
  443.1 65.8 %all-gather.5.cloned.1.call-done = bf16[256,2048]{1,0:T(8,128)(2,1)} async-done(((bf16[8,2048]{1,0:T(8,128)(2,1)}), bf16[256,2048]{1,0:T(8,128)(2,1)}) %all-gather.5.cloned.1.call-update) | async-done | bytes 1048592 | tf_op jit(solution)/shard_map/all_gather | solution.py:134
  508.9 2.2 convolution_convert_fusion
  511.1 1.3 dynamic-slice
  513.1 132.5 %all-reduce.9.cloned.1.call-done = bf16[256,1664]{1,0:T(8,128)(2,1)} async-done(((bf16[256,1664]{1,0:T(8,128)(2,1)}), bf16[256,1664]{1,0:T(8,128)(2,1)}) %all-reduce.9.cloned.1.call-update) | async-done | bytes 851984
  645.6 0.7 dynamic-slice_convert_fusion
  646.4 2.3 collective-permute-start
  648.7 0.8 collective-permute-done
  649.6 0.6 copy.26
  (64 shorter events, 2.6 us)
Async XLA Ops:
  6.5 2.5 copy-start
  6.5 4.8 copy-start.9
  6.5 3.9 copy-start.5
  6.5 4.2 copy-start.11
  6.5 5.6 copy-start.3
  6.5 134.5 %all-reduce.5.cloned.1.call-start = ((), (), s32[]{:S(2)}) async-start(), calls=%async_computation.1 | async-start | bytes 131072 | tf_op jit(solution)/shard_map/psum | solution.py:112
  9.1 131.9 %copy-start.4 = (bf16[1,8,2048]{2,1,0:T(8,128)(2,1)S(1)}, bf16[1,8,2048]{2,1,0:T(8,128)(2,1)}, u32[]{:S(2)}) copy-start(bf16[1,8,2048]{2,1,0:T(8,128)(2,1)} %param.12) | copy-start | bytes 98308
  9.1 133.7 %copy-start.7 = (s32[2,128,8]{1,2,0:T(8,128)S(1)}, s32[2,128,8]{1,2,0:T(8,128)}, u32[]{:S(2)}) copy-start(s32[2,128,8]{1,2,0:T(8,128)} %param.18) | copy-start | bytes 24580
  10.3 132.6 %copy-start.8 = (f32[2,128,8]{1,2,0:T(8,128)S(1)}, f32[2,128,8]{1,2,0:T(8,128)}, u32[]{:S(2)}) copy-start(f32[2,128,8]{1,2,0:T(8,128)} %param.19) | copy-start | bytes 24580
  12.1 199.8 %copy-start.2 = (bf16[128,2048]{1,0:T(8,128)(2,1)S(1)}, bf16[128,2048]{1,0:T(8,128)(2,1)}, u32[]{:S(2)}) copy-start(bf16[128,2048]{1,0:T(8,128)(2,1)} %param.21) | copy-start | bytes 1572868
  13.0 197.0 %all-gather.3.cloned.1.call-start = ((), (), s32[]{:S(2)}) async-start(), calls=%async_computation.2 | async-start | bytes 1081344 | tf_op jit(solution)/shard_map/all_gather | solution.py:126
  142.7 171.9 %reduce-scatter.2.cloned.1.call-start = ((), (), s32[]{:S(2)}) async-start(), calls=%async_computation.3 | async-start | bytes 2162688 | tf_op jit(solution)/shard_map/reduce_scatter | solution.py:131
  210.0 1.9 copy-start.1
  215.1 293.8 %copy-start.6 = (bf16[64,1664]{1,0:T(8,128)(2,1)S(1)}, bf16[64,1664]{1,0:T(8,128)(2,1)}, u32[]{:S(2)}) copy-start(bf16[64,1664]{1,0:T(8,128)(2,1)} %param.22) | copy-start | bytes 638980
  215.1 434.4 %copy-start.10 = (f32[8]{0:T(128)S(1)}, f32[8]{0:T(128)}, u32[]{:S(2)}) copy-start(f32[8]{0:T(128)} %param.23) | copy-start | bytes 100
  215.1 225.4 %all-reduce.7.cloned.1.call-start = ((), (), s32[]{:S(2)}) async-start(), calls=%async_computation.4 | async-start | bytes 131072 | tf_op jit(solution)/shard_map/psum | solution.py:132
  314.6 194.3 %all-gather.5.cloned.1.call-start = ((), (), s32[]{:S(2)}) async-start(), calls=%async_computation.5 | async-start | bytes 1081344 | tf_op jit(solution)/shard_map/all_gather | solution.py:134
  443.1 202.6 %all-reduce.9.cloned.1.call-start = ((), (), s32[]{:S(2)}) async-start(), calls=%async_computation.6 | async-start | bytes 1703936
  646.4 3.1 collective-permute-start
Sparse Core Ops, SparseCore 0:
  13.1 127.8 all-reduce.4
  144.7 65.3 all-gather.2
  215.3 99.2 reduce-scatter.1
  316.9 123.6 all-reduce.6
  443.6 65.3 all-gather.4
  512.1 133.5 all-reduce.8
where the time goes:
time: 658 us; the launch traced here: 657 us
  waiting for transfers between devices  618 us (94%)
  between operations  14.4 us (2%)
  matrix products  9.92 us (2%)
  other arithmetic  9.7 us (1%)
    unnamed x7, waiting for transfers between devices  133 us
    psum x1, waiting for transfers between devices, body(): attention_out = lax.psum(partial_out, 'mp')  128 us
    psum x1, waiting for transfers between devices, body(): expert_total = lax.psum(expert_part, 'mp')  126 us
    reduce_scatter x1, waiting for transfers between devices, body(): lax.psum_scatter(expert_terms, ('guide', 'dp'), scatter_dimension=0, tile...  99.4 us
    all_gather x1, waiting for transfers between devices, body(): final_all = lax.all_gather(final, ('guide', 'dp'), axis=0, tiled=True)  65.8 us
    all_gather x1, waiting for transfers between devices, body(): piece = lax.all_gather(moe_in, ('guide', 'dp'), axis=0, tiled=True)  65.6 us
  transfers between devices with their start and end apart: 7, of which 7 were waited for; matrix products, arithmetic and copies ran while one was open for 0% of the time, Pallas kernels for 0%

commit v1 on v0

--- a/solution.py
+++ b/solution.py
@@ -109,7 +109,7 @@
         + self_prob[..., None].astype(jnp.float32) * fresh_value.astype(jnp.float32)
     ).astype(jnp.bfloat16)
     partial_out = jnp.einsum("rhe,hed->rd", mixture, out_weight, preferred_element_type=jnp.float32)
-    attention_out = lax.psum(partial_out, "mp")
+    attention_out = jnp.sum(lax.all_gather(partial_out, "mp"), axis=0)
     residual = (hidden.astype(jnp.float32) + attention_out).astype(jnp.bfloat16)
     moe_in = rms_norm(residual.astype(jnp.float32)).astype(jnp.bfloat16)
     unit_count = expert_in.shape[2]

time: 658 us -> 596 us (0.906)
  waiting for transfers between devices: 618 us -> 556 us
    psum x1 -> x0, waiting for transfers between devices: 128 us -> none  [body(): attention_out = lax.psum(partial_out, 'mp')]
    all_gather x0 -> x1, waiting for transfers between devices: none -> 67 us  [body(): attention_out = jnp.sum(lax.all_gather(partial_out, 'mp'), axis=0)]
where the time goes in v1:
time: 596 us
  waiting for transfers between devices  556 us (93%)
  between operations  14.3 us (2%)
  other arithmetic  10.1 us (2%)
  matrix products  9.87 us (2%)
    unnamed x7, waiting for transfers between devices  133 us
    psum x1, waiting for transfers between devices, body(): expert_total = lax.psum(expert_part, 'mp')  126 us
    reduce_scatter x1, waiting for transfers between devices, body(): lax.psum_scatter(expert_terms, ('guide', 'dp'), scatter_dimension=0, tile...  99.3 us
    all_gather x1, waiting for transfers between devices, body(): attention_out = jnp.sum(lax.all_gather(partial_out, 'mp'), axis=0)  67 us
    all_gather x1, waiting for transfers between devices, body(): final_all = lax.all_gather(final, ('guide', 'dp'), axis=0, tiled=True)  66.3 us
    all_gather x1, waiting for transfers between devices, body(): piece = lax.all_gather(moe_in, ('guide', 'dp'), axis=0, tiled=True)  64.2 us
  transfers between devices with their start and end apart: 7, of which 7 were waited for; matrix products, arithmetic and copies ran while one was open for 0% of the time, Pallas kernels for 0%

profile of v1, /device:TPU:1, one launch (start us, length us, event | category | flops | bytes accessed | tf_op | source)
XLA Modules:
  0.0 595.8 jit_solution(16228075824114601059)
XLA Ops:
  6.6 0.8 bitcast_convert_fusion
  7.4 0.8 broadcast_subtract_fusion
  8.2 0.9 fusion.23
  9.1 1.1 fusion
  12.0 0.9 fusion.11
  13.0 67.0 %all-gather.9.cloned.1.call-done = f32[128,2048]{1,0:T(8,128)} async-done(((f32[8,2048]{1,0:T(8,128)}), f32[128,2048]{1,0:T(8,128)}) %all-gather.9.cloned.1.call-update) | async-done | bytes 1048592 | tf_op jit(solution)/shard_map/all_gather | solution.py:112
  80.0 1.3 bitcast_reduce_fusion
  81.4 0.7 fusion.27
  82.5 1.3 select_reduce_fusion
  83.8 64.2 %all-gather.5.cloned.1.call-done = bf16[256,2048]{1,0:T(8,128)(2,1)} async-done(((bf16[8,2048]{1,0:T(8,128)(2,1)}), bf16[256,2048]{1,0:T(8,128)(2,1)}) %all-gather.5.cloned.1.call-update) | async-done | bytes 1048592 | tf_op jit(solution)/shard_map/all_gather | solution.py:126
  148.0 1.9 fusion.9
  149.9 3.2 fusion.4
  153.2 99.3 %reduce-scatter.2.cloned.1.call-done = f32[8,2048]{1,0:T(8,128)} async-done(((f32[256,2048]{1,0:T(8,128)}), f32[8,2048]{1,0:T(8,128)}) %reduce-scatter.2.cloned.1.call-update) | async-done | bytes 65552 | tf_op jit(solution)/shard_map/reduce_scatter | solution.py:131
  252.6 125.8 %all-reduce.4.cloned.1.call-done = f32[8,2048]{1,0:T(8,128)} async-done(((f32[8,2048]{1,0:T(8,128)}), f32[8,2048]{1,0:T(8,128)}) %all-reduce.4.cloned.1.call-update) | async-done | bytes 65552 | tf_op jit(solution)/shard_map/psum | solution.py:132
  378.4 1.0 multiply_reduce_fusion
  379.4 1.5 multiply_convert_fusion
  381.0 66.3 %all-gather.7.cloned.1.call-done = bf16[256,2048]{1,0:T(8,128)(2,1)} async-done(((bf16[8,2048]{1,0:T(8,128)(2,1)}), bf16[256,2048]{1,0:T(8,128)(2,1)}) %all-gather.7.cloned.1.call-update) | async-done | bytes 1048592 | tf_op jit(solution)/shard_map/all_gather | solution.py:134
  447.3 2.2 convolution_convert_fusion
  449.5 1.3 dynamic-slice
  451.4 132.9 %all-reduce.6.cloned.1.call-done = bf16[256,1664]{1,0:T(8,128)(2,1)} async-done(((bf16[256,1664]{1,0:T(8,128)(2,1)}), bf16[256,1664]{1,0:T(8,128)(2,1)}) %all-reduce.6.cloned.1.call-update) | async-done | bytes 851984
  584.3 0.7 dynamic-slice_convert_fusion
  585.1 2.3 collective-permute-start
  587.4 0.8 collective-permute-done
  588.3 0.6 copy.26
  (65 shorter events, 2.7 us)
Async XLA Ops:
  6.5 2.5 copy-start
  6.5 4.7 copy-start.9
  6.5 3.9 copy-start.5
  6.5 4.1 copy-start.11
  6.5 5.5 copy-start.3
  6.5 73.4 %all-gather.9.cloned.1.call-start = ((), (), s32[]{:S(2)}) async-start(), calls=%async_computation.5 | async-start | bytes 1114112 | tf_op jit(solution)/shard_map/all_gather | solution.py:112
  10.2 71.0 %copy-start.4 = (bf16[1,8,2048]{2,1,0:T(8,128)(2,1)S(1)}, bf16[1,8,2048]{2,1,0:T(8,128)(2,1)}, u32[]{:S(2)}) copy-start(bf16[1,8,2048]{2,1,0:T(8,128)(2,1)} %param.12) | copy-start | bytes 98308
  10.4 71.8 %copy-start.7 = (s32[2,128,8]{1,2,0:T(8,128)S(1)}, s32[2,128,8]{1,2,0:T(8,128)}, u32[]{:S(2)}) copy-start(s32[2,128,8]{1,2,0:T(8,128)} %param.18) | copy-start | bytes 24580
  10.6 71.7 %copy-start.8 = (f32[2,128,8]{1,2,0:T(8,128)S(1)}, f32[2,128,8]{1,2,0:T(8,128)}, u32[]{:S(2)}) copy-start(f32[2,128,8]{1,2,0:T(8,128)} %param.19) | copy-start | bytes 24580
  12.9 135.1 %all-gather.5.cloned.1.call-start = ((), (), s32[]{:S(2)}) async-start(), calls=%async_computation.1 | async-start | bytes 1081344 | tf_op jit(solution)/shard_map/all_gather | solution.py:126
  81.2 68.6 %copy-start.2 = (bf16[128,2048]{1,0:T(8,128)(2,1)S(1)}, bf16[128,2048]{1,0:T(8,128)(2,1)}, u32[]{:S(2)}) copy-start(bf16[128,2048]{1,0:T(8,128)(2,1)} %param.21) | copy-start | bytes 1572868
  82.1 170.4 %reduce-scatter.2.cloned.1.call-start = ((), (), s32[]{:S(2)}) async-start(), calls=%async_computation.2 | async-start | bytes 2162688 | tf_op jit(solution)/shard_map/reduce_scatter | solution.py:131
  148.0 1.9 copy-start.1
  153.1 294.2 %copy-start.6 = (bf16[64,1664]{1,0:T(8,128)(2,1)S(1)}, bf16[64,1664]{1,0:T(8,128)(2,1)}, u32[]{:S(2)}) copy-start(bf16[64,1664]{1,0:T(8,128)(2,1)} %param.22) | copy-start | bytes 638980
  153.1 435.1 %copy-start.10 = (f32[8]{0:T(128)S(1)}, f32[8]{0:T(128)}, u32[]{:S(2)}) copy-start(f32[8]{0:T(128)} %param.23) | copy-start | bytes 100
  153.1 225.3 %all-reduce.4.cloned.1.call-start = ((), (), s32[]{:S(2)}) async-start(), calls=%async_computation.3 | async-start | bytes 131072 | tf_op jit(solution)/shard_map/psum | solution.py:132
  252.5 194.7 %all-gather.7.cloned.1.call-start = ((), (), s32[]{:S(2)}) async-start(), calls=%async_computation.4 | async-start | bytes 1081344 | tf_op jit(solution)/shard_map/all_gather | solution.py:134
  380.9 203.4 %all-reduce.6.cloned.1.call-start = ((), (), s32[]{:S(2)}) async-start(), calls=%async_computation.6 | async-start | bytes 1703936
  585.1 3.1 collective-permute-start
Sparse Core Ops, SparseCore 0:
  13.0 66.8 all-gather.8
  83.1 64.8 all-gather.4
  153.2 99.2 reduce-scatter.1
  254.7 123.6 all-reduce.3
  381.9 65.3 all-gather.6
  450.8 133.5 all-reduce.5
